TPU v7x, 768 devices: a whole 4x8x12 slice. The times are simulated.
768 devices in a mesh: ctx: 12 (over z), head: 64 (over x, y, core).
Axes of the slice: x: 4, y: 8, z: 12, core: 2. Of those that a mesh axis runs over, the one named last changes fastest.
Arguments:
- queries: bfloat16 [24576, 8192], P('ctx', 'head'), may hold values from -6 to 6
- keys: bfloat16 [24576, 8192], P('ctx', 'head'), may hold values from -0.5 to 0.5
- values: bfloat16 [24576, 8192], P('ctx', 'head'), may hold values from -24 to 24
- norm_gain: float32 [8192], P('head'), may hold values from 0.1 to 1.9
- out_grad: bfloat16 [24576, 8192], P('ctx', 'head'), may hold values from -6 to 6
Outputs:
- query_grad: bfloat16 [24576, 8192], P('ctx', 'head')
- key_grad: bfloat16 [24576, 8192], P('ctx', 'head')
- value_grad: bfloat16 [24576, 8192], P('ctx', 'head')
All inputs are finite; a program needn't handle non-finite values.
Results may differ from a plain program's by a relative error of at most 0.005.
Values sent between devices are 32-bit elements; how exact they have to be, the bound alone decides.
A program may use at most 32 MiB of HBM per device.

v0:
```python
import jax
import jax.numpy as jnp
from jax import lax
from jax.sharding import PartitionSpec as P

HEAD_DIM = 128
GROUP = 512


HIGH = lax.Precision.HIGHEST


def add_lower(mine, piece):
    place = jnp.arange(piece.shape[0], dtype=jnp.int32)
    weight = (place < mine).astype(jnp.float32)
    return jnp.sum(piece * weight[:, None, None, None], axis=0)


def add_upper(mine, piece):
    place = jnp.arange(piece.shape[0], dtype=jnp.int32)
    weight = (place > mine).astype(jnp.float32)
    return jnp.sum(piece * weight[:, None, None, None], axis=0)


def per_device(queries, keys, values, norm_gain, out_grad):
    tokens_here = queries.shape[0]
    head_dim = HEAD_DIM
    heads_here = queries.shape[1] // head_dim
    blocks = tokens_here // GROUP
    width = lax.axis_size("head") * heads_here * head_dim
    mine = lax.axis_index("ctx")
    q4 = queries.reshape(blocks, GROUP, heads_here, head_dim)
    k4 = keys.reshape(blocks, GROUP, heads_here, head_dim)
    v4 = values.reshape(blocks, GROUP, heads_here, head_dim)
    gain = norm_gain.reshape(1, 1, heads_here, head_dim)
    upart = out_grad.reshape(blocks, GROUP, heads_here, head_dim).astype(jnp.float32) * gain
    causal = jnp.tril(jnp.ones((GROUP, GROUP), jnp.float32))
    block_kv = jnp.einsum("nshd,nshe->nhde", k4, v4, preferred_element_type=jnp.float32)
    local_kv = jnp.sum(block_kv, axis=0)
    earlier = add_lower(mine, lax.all_gather(local_kv[None], "ctx", axis=0, tiled=True))
    state = earlier[None] + jnp.cumsum(block_kv, axis=0) - block_kv
    scores = (
        jnp.einsum("nchd,nshd->nhcs", q4, k4, preferred_element_type=jnp.float32) * causal
    ).astype(jnp.bfloat16)
    attended = jnp.einsum("nhcs,nshe->nche", scores, v4, preferred_element_type=jnp.float32)
    attended = attended + jnp.einsum(
        "nchd,nhde->nche", q4.astype(jnp.float32), state, precision=HIGH
    )
    power_part = jnp.sum(attended * attended, axis=(2, 3))
    cross_part = jnp.sum(attended * upart, axis=(2, 3))
    power, cross = lax.psum((power_part, cross_part), "head")
    ratio = lax.rsqrt(power / width + 1e-06)
    agrad = (
        ratio[:, :, None, None] * upart - attended * (ratio**3 * (cross / width))[:, :, None, None]
    ).astype(jnp.bfloat16)
    backflow = (
        jnp.einsum("nche,nshe->nhcs", agrad, v4, preferred_element_type=jnp.float32) * causal
    ).astype(jnp.bfloat16)
    qgrad = jnp.einsum("nhcs,nshd->nchd", backflow, k4, preferred_element_type=jnp.float32)
    qgrad = qgrad + jnp.einsum("nche,nhde->nchd", agrad.astype(jnp.float32), state, precision=HIGH)
    block_adj = jnp.einsum("nchd,nche->nhde", q4, agrad, preferred_element_type=jnp.float32)
    local_adj = jnp.sum(block_adj, axis=0)
    later = add_upper(mine, lax.all_gather(local_adj[None], "ctx", axis=0, tiled=True))
    adjoint = later[None] + local_adj[None] - jnp.cumsum(block_adj, axis=0)
    kgrad = jnp.einsum("nhcs,nchd->nshd", backflow, q4, preferred_element_type=jnp.float32)
    kgrad = kgrad + jnp.einsum("nshe,nhde->nshd", v4.astype(jnp.float32), adjoint, precision=HIGH)
    vgrad = jnp.einsum("nhcs,nche->nshe", scores, agrad, preferred_element_type=jnp.float32)
    vgrad = vgrad + jnp.einsum("nshd,nhde->nshe", k4.astype(jnp.float32), adjoint, precision=HIGH)
    shape_out = (tokens_here, heads_here * head_dim)
    return (
        qgrad.reshape(shape_out).astype(jnp.bfloat16),
        kgrad.reshape(shape_out).astype(jnp.bfloat16),
        vgrad.reshape(shape_out).astype(jnp.bfloat16),
    )


def solution(mesh):
    return jax.shard_map(
        per_device,
        mesh=mesh,
        in_specs=(
            P("ctx", "head"),
            P("ctx", "head"),
            P("ctx", "head"),
            P("head"),
            P("ctx", "head"),
        ),
        out_specs=(P("ctx", "head"), P("ctx", "head"), P("ctx", "head")),
        check_vma=False,
    )
```

profile of v0, /device:TPU:64, one launch (start us, length us, event | category | flops | bytes accessed | tf_op | source)
XLA Modules:
  0.0 334.3 jit_solution(16359154667372189541)
XLA Ops:
  0.6 0.0 copy-start
  0.6 0.0 copy-start.10
  0.7 1.0 copy-done
  1.7 1.5 fusion.9
  3.2 34.0 %all-gather = f32[1536,128]{1,0:T(8,128)S(1)} all-gather(f32[128,128]{1,0:T(8,128)S(1)} %get-tuple-element.9), channel_id=2, replica_groups=mesh['ctx'=12,'head'=64] {'ctx'}, dimensions={0}, use_global_device_ids=true | all-gather | bytes 851968 | tf_op jit(solution)/shard_map/all_gather | solution.py:40
  37.2 0.0 copy-start.4
  37.2 0.1 multiply_reduce_fusion.3
  37.4 0.0 copy-done.10
  37.4 1.2 copy.57
  38.6 0.1 fusion.6
  38.8 0.0 copy-done.4
  38.8 0.0 copy-start.2
  38.8 0.0 copy-start.6
  38.8 0.7 multiply_convert_fusion.1
  39.5 0.2 copy-done.2
  39.8 0.4 copy-done.6
  40.2 0.0 copy-start.1
  40.2 0.0 copy-start.11
  40.2 0.8 convolution_bitcast_fusion.2
  41.0 0.4 copy-done.1
  41.4 0.0 copy-done.11
  41.4 1.8 multiply_reduce_fusion.1
  43.2 246.9 %all-reduce = (f32[4,512]{1,0:T(4,128)S(1)}, f32[4,512]{1,0:T(4,128)S(1)}) all-reduce(f32[4,512]{1,0:T(4,128)S(1)} %get-tuple-element.4, f32[4,512]{1,0:T(4,128)S(1)} %get-tuple-element.3), channel_id=1, replica_groups=mesh['ctx'=12,'head'=64] {'head'}, use_global_device_ids=true, to_apply=%region_6.7 | all-reduce | flops 4096 | bytes 32768 | tf_op jit(solution)/shard_map/psum | solution.py:51
  290.1 1.8 fusion.7
  291.9 1.5 fusion.11
  293.4 1.0 fusion.10
  294.4 0.0 copy-start.5
  294.4 27.6 %all-gather.1 = f32[1536,128]{0,1:T(8,128)S(1)} all-gather(f32[128,128]{0,1:T(8,128)S(1)} %get-tuple-element.12), channel_id=3, replica_groups=mesh['ctx'=12,'head'=64] {'ctx'}, dimensions={0}, use_global_device_ids=true | all-gather | bytes 851968 | tf_op jit(solution)/shard_map/all_gather | solution.py:63
  322.0 0.3 copy.62
  322.3 0.1 multiply_reduce_fusion.2
  322.4 0.1 copy.63
  322.5 0.0 copy-start.3
  322.5 0.0 copy-start.7
  322.5 1.1 reduce-window_subtract_fusion
  323.6 0.0 copy-start.8
  323.6 0.7 copy-done.8
  324.4 0.0 copy-done.5
  324.4 2.6 fusion.4
  327.0 2.0 copy.66
  329.0 0.0 copy-done.3
  329.0 0.0 copy-done.7
  329.0 0.8 multiply_convert_fusion
  329.8 0.9 convolution_bitcast_fusion
  330.7 0.7 convolution_bitcast_fusion.1
  331.4 0.0 copy-start.9
  331.4 1.5 fusion.1
  332.9 0.0 copy-done.9
  332.9 1.4 fusion.2
  (5 shorter events, 0.1 us)
Async XLA Ops:
  0.6 1.0 copy-start
  0.6 36.7 %copy-start.10 = (bf16[2048,128]{1,0:T(8,128)(2,1)S(1)}, bf16[2048,128]{1,0:T(8,128)(2,1)}, u32[]{:S(2)}) copy-start(bf16[2048,128]{1,0:T(8,128)(2,1)} %param.9) | copy-start | bytes 1572868
  37.2 1.5 copy-start.4
  38.8 1.0 copy-start.2
  38.8 1.4 copy-start.6
  40.2 1.2 copy-start.1
  40.2 1.2 copy-start.11
  294.4 30.0 %copy-start.5 = (bf16[2048,128]{1,0:T(8,128)(2,1)S(1)}, bf16[2048,128]{1,0:T(8,128)(2,1)}, u32[]{:S(2)}) copy-start(bf16[2048,128]{1,0:T(8,128)(2,1)} %param.6) | copy-start | bytes 1572868
  322.5 6.5 %copy-start.3 = (f32[512,512]{1,0:T(8,128)S(1)}, f32[512,512]{1,0:T(8,128)}, u32[]{:S(2)}) copy-start(f32[512,512]{1,0:T(8,128)} %copy-done.2) | copy-start | bytes 3145732
  322.5 6.5 %copy-start.7 = (bf16[2048,128]{1,0:T(8,128)(2,1)S(1)}, bf16[2048,128]{1,0:T(8,128)(2,1)}, u32[]{:S(2)}) copy-start(bf16[2048,128]{1,0:T(8,128)(2,1)} %param.7) | copy-start | bytes 1572868
  323.6 0.7 copy-start.8
  331.4 1.5 copy-start.9
where the time goes:
time: 335 us; the launch traced here: 334 us
  blocking collectives  308 us (92%)
  matrix products  15.2 us (5%)
  local copies, waits for them, and re-layouts  6.49 us (2%)
    psum x1, blocking collectives, per_device(): power, cross = lax.psum((power_part, cross_part), 'head')  247 us
    all_gather x1, blocking collectives, per_device(): lax.all_gather(local_kv[None], 'ctx', axis=0, tiled=True)  34 us
    all_gather x1, blocking collectives, per_device(): lax.all_gather(local_adj[None], 'ctx', axis=0, tiled=True)  27.6 us

commit v1 on v0

v1 whole, which is shorter than its diff:
```python
import jax
import jax.numpy as jnp
from jax import lax
from jax.experimental import pallas as pl
from jax.experimental.pallas import tpu as pltpu
from jax.sharding import PartitionSpec as P

HEAD_DIM = 128
GROUP = 512
NZ = 12
NX, NY, NC = 4, 8, 2
NM = NX * NC
ARC = 4
ROWS = HEAD_DIM // ARC
MESH = pl.DeviceIdType.MESH
F32 = jnp.float32
BF16 = jnp.bfloat16
FAR_FIRST = (6, 5, 7, 4, 8, 3, 9, 2, 10, 1, 11)
NEAR = (2, 1, -1)


def dot(a, b):
    return lax.dot_general(a, b, (((1,), (0,)), ((), ())), preferred_element_type=F32)


def dot_nt(a, b):
    return lax.dot_general(a, b, (((1,), (1,)), ((), ())), preferred_element_type=F32)


def split(x):
    hi = x.astype(BF16)
    return hi, (x - hi.astype(F32)).astype(BF16)


class Scan:
    def __init__(self, z, head, earlier, refs):
        self.z, self.head, self.earlier = z, head, earlier
        self.src, self.near, self.out, self.inb, self.s1, self.r1, self.s2, self.r2 = refs

    def before(self, i, j):
        return i < j if self.earlier else i > j

    def first(self):
        copies = []
        for n, off in enumerate(NEAR):
            to = (self.z + off + NZ) % NZ
            copies.append(pltpu.make_async_remote_copy(
                src_ref=self.src.at[to % ARC], dst_ref=self.near.at[n],
                send_sem=self.s1.at[n], recv_sem=self.r1.at[n],
                device_id=(to, self.head), device_id_type=MESH))
        return copies

    def second(self):
        copies = []
        for t in FAR_FIRST:
            to = (self.z + t) % NZ
            copies.append(pltpu.make_async_remote_copy(
                src_ref=self.out.at[t], dst_ref=self.inb.at[t],
                send_sem=self.s2.at[t], recv_sem=self.r2.at[t],
                device_id=(to, self.head), device_id_type=MESH))
        return copies

    def start(self):
        self.c1 = self.first()
        for copy in self.c1:
            copy.start()

    def forward(self):
        for copy in self.c1:
            copy.wait()
        mine = [(self.z, self.src[self.z % ARC])]
        for n, off in enumerate(NEAR):
            mine.append(((self.z - off + NZ) % NZ, self.near[n]))
        self.c2 = self.second()
        for n, t in enumerate((*FAR_FIRST, 0)):
            to = (self.z + t) % NZ
            total = jnp.zeros((ROWS, HEAD_DIM), F32)
            for i, piece in mine:
                total = total + jnp.where(self.before(i, to), piece, 0.0)
            self.out[t] = total
            if t:
                self.c2[n].start()

    def finish(self, result):
        for copy in self.c2:
            copy.wait()
        for r in range(ARC):
            first = self.out[0] if r == 0 else self.inb[r]
            result[(self.z - r + NZ) % ARC] = first + self.inb[r + 4] + (self.inb[r + 8])


def kernel(blocks, width, q_hbm, k_hbm, v_hbm, gain_ref, og_hbm, qg_hbm, kg_hbm, vg_hbm,
           q, k, v, og, qg, kg, vg, vt, kt, ut, at, sct, agt, ag, kgf, vgf,
           kvt, sth, stl, st, stdh, stdl, adj, ext,
           src1, near1, out1, in1, src2, near2, out2, in2,
           stat, mstat, xin, yin,
           lsem, osem, s11, r11, s12, r12, s21, r21, s22, r22, sx, rx, sy, ry):
    z = lax.axis_index("ctx")
    head = lax.axis_index("head")
    core = head % NC
    y = (head // NC) % NY
    x = head // (NC * NY)
    m = x * NC + core

    loads = [pltpu.make_async_copy(a, b, lsem.at[n])
             for n, (a, b) in enumerate(((k_hbm, k), (v_hbm, v), (q_hbm, q), (og_hbm, og)))]
    for copy in loads:
        copy.start()

    barrier = pltpu.get_barrier_semaphore()
    xpeers, ypeers = [], []
    for d in range(1, NM):
        to = (m + d) % NM
        xpeers.append(((to // NC) * NY + y) * NC + to % NC)
    for d in range(1, NY):
        ypeers.append((x * NY + (y + d) % NY) * NC + core)
    for t in FAR_FIRST:
        pl.semaphore_signal(barrier, inc=1, device_id=((z + t) % NZ, head), device_id_type=MESH)
    for to in ypeers + xpeers:
        pl.semaphore_signal(barrier, inc=1, device_id=(z, to), device_id_type=MESH)

    loads[0].wait()
    loads[1].wait()
    total = jnp.zeros((HEAD_DIM, HEAD_DIM), F32)
    for n in range(blocks):
        vt[n] = v[n].T
        kvt[n] = total
        total = total + dot(vt[n], k[n])
    src1[...] = total.reshape(ARC, ROWS, HEAD_DIM)

    pl.semaphore_wait(barrier, NZ - 1 + NM - 1 + NY - 1)
    scan1 = Scan(z, head, True, (src1, near1, out1, in1, s11, r11, s12, r12))
    scan1.start()

    row = lax.broadcasted_iota(jnp.int32, (GROUP, GROUP), 0)
    col = lax.broadcasted_iota(jnp.int32, (GROUP, GROUP), 1)
    keep = row <= col
    gain = gain_ref[...]

    def local_scores(n):
        sct[n] = jnp.where(keep, dot_nt(k[n], q[n]), 0.0).astype(BF16)
        at[n] = dot(vt[n], sct[n])

    def local_rest(n):
        ut[n] = (og[n].astype(F32) * gain).T
        kt[n] = k[n].T

    loads[2].wait()
    loads[3].wait()
    for n in range(blocks // 2):
        local_scores(n)
    scan1.forward()
    for n in range(blocks // 2, blocks):
        local_scores(n)
    for n in range(blocks):
        local_rest(n)
    scan1.finish(ext)

    tiles = GROUP // HEAD_DIM
    earlier = ext[...].reshape(HEAD_DIM, HEAD_DIM)
    xcopies, ycopies = [], {}
    for n in range(blocks):
        state = earlier + kvt[n]
        st[n] = state
        hi, lo = split(state)
        a = at[n] + dot_nt(hi, q[n]) + dot_nt(lo, q[n])
        at[n] = a
        power = jnp.sum(a * a, axis=0, keepdims=True)
        cross = jnp.sum(a * ut[n], axis=0, keepdims=True)
        for c in range(tiles):
            stat[n, c : c + 1, :] = power[:, c * HEAD_DIM : (c + 1) * HEAD_DIM]
            stat[n, tiles + c : tiles + c + 1, :] = cross[:, c * HEAD_DIM : (c + 1) * HEAD_DIM]
        for d in range(1, NM):
            copy = pltpu.make_async_remote_copy(
                src_ref=stat.at[n], dst_ref=xin.at[n, d - 1],
                send_sem=sx.at[n, d - 1], recv_sem=rx.at[n, d - 1],
                device_id=(z, xpeers[d - 1]), device_id_type=MESH)
            copy.start()
            xcopies.append(copy)
    for n in range(blocks):
        total = stat[n]
        for d in range(1, NM):
            xcopies[n * (NM - 1) + d - 1].wait()
            total = total + xin[n, d - 1]
        mstat[n] = total
        for d in sorted(range(1, NY), key=lambda d: -min(d, NY - d)):
            copy = pltpu.make_async_remote_copy(
                src_ref=mstat.at[n], dst_ref=yin.at[n, d - 1],
                send_sem=sy.at[n, d - 1], recv_sem=ry.at[n, d - 1],
                device_id=(z, ypeers[d - 1]), device_id_type=MESH)
            copy.start()
            ycopies[n, d] = copy
    for n in range(blocks):
        stdh[n], stdl[n] = split(st[n].T)
    suffix = jnp.zeros((HEAD_DIM, HEAD_DIM), F32)
    for n in range(blocks):
        total = mstat[n]
        for d in range(1, NY):
            ycopies[n, d].wait()
            total = total + yin[n, d - 1]
        ratio = lax.rsqrt(total[:tiles] / width + 1e-06)
        scale = ratio * ratio * ratio * (total[tiles:] / width)
        for c in range(tiles):
            part = slice(c * HEAD_DIM, (c + 1) * HEAD_DIM)
            agt[n, :, part] = (ratio[c : c + 1] * ut[n, :, part] - at[n, :, part] * scale[c : c + 1]).astype(BF16)
        adj[n] = dot(agt[n], q[n])
    for n in reversed(range(blocks)):
        own = adj[n]
        adj[n] = suffix
        suffix = suffix + own
    src2[...] = suffix.reshape(ARC, ROWS, HEAD_DIM)
    scan2 = Scan(z, head, False, (src2, near2, out2, in2, s21, r21, s22, r22))
    scan2.start()

    def local_grads(n):
        bft = jnp.where(keep, dot(v[n], agt[n]), 0.0).astype(BF16)
        qgt = dot(kt[n], bft) + dot(stdh[n], agt[n]) + dot(stdl[n], agt[n])
        qg[n] = qgt.T.astype(BF16)
        kgf[n] = dot(bft, q[n])
        ag[n] = agt[n].T
        vgf[n] = dot(sct[n], ag[n])

    for n in range(blocks // 2):
        local_grads(n)
    scan2.forward()
    for n in range(blocks // 2, blocks):
        local_grads(n)
    out_q = pltpu.make_async_copy(qg, qg_hbm, osem.at[0])
    out_q.start()
    scan2.finish(ext)
    later = ext[...].reshape(HEAD_DIM, HEAD_DIM)
    for n in range(blocks):
        hi, lo = split(later + adj[n])
        kg[n] = (kgf[n] + dot(v[n], hi) + dot(v[n], lo)).astype(BF16)
        vg[n] = (vgf[n] + dot_nt(k[n], hi) + dot_nt(k[n], lo)).astype(BF16)
    out_k = pltpu.make_async_copy(kg, kg_hbm, osem.at[1])
    out_v = pltpu.make_async_copy(vg, vg_hbm, osem.at[2])
    out_k.start()
    out_v.start()
    out_q.wait()
    out_k.wait()
    out_v.wait()


def per_device(queries, keys, values, norm_gain, out_grad):
    tokens = queries.shape[0]
    blocks = tokens // GROUP
    width = lax.axis_size("head") * HEAD_DIM
    nat = (blocks, GROUP, HEAD_DIM)
    tra = (blocks, HEAD_DIM, GROUP)
    sq = (blocks, HEAD_DIM, HEAD_DIM)
    V = pltpu.VMEM
    D = pltpu.SemaphoreType.DMA
    piece = (ROWS, HEAD_DIM)
    srows = 2 * GROUP // HEAD_DIM
    zbuf = [V((ARC, *piece), F32), V((len(NEAR), *piece), F32), V((NZ, *piece), F32), V((NZ, *piece), F32)]
    zsem = [D((len(NEAR),)), D((len(NEAR),)), D((NZ,)), D((NZ,))]
    anyspec = pl.BlockSpec(memory_space=pl.ANY)
    out = pl.pallas_call(
        lambda *refs: kernel(blocks, width, *refs),
        out_shape=[jax.ShapeDtypeStruct(nat, BF16)] * 3,
        in_specs=[anyspec] * 3 + [pl.BlockSpec(memory_space=pltpu.VMEM)] + [anyspec],
        out_specs=[anyspec] * 3,
        scratch_shapes=[V(nat, BF16)] * 7
        + [V(tra, BF16), V(tra, BF16), V(tra, F32), V(tra, F32), V((blocks, GROUP, GROUP), BF16),
           V(tra, BF16), V(nat, BF16), V(nat, F32), V(nat, F32),
           V(sq, F32), V(sq, BF16), V(sq, BF16), V(sq, F32), V(sq, BF16), V(sq, BF16), V(sq, F32),
           V((ARC, *piece), F32)]
        + zbuf + zbuf
        + [V((blocks, srows, HEAD_DIM), F32), V((blocks, srows, HEAD_DIM), F32),
           V((blocks, NM - 1, srows, HEAD_DIM), F32), V((blocks, NY - 1, srows, HEAD_DIM), F32)]
        + [D((4,)), D((3,))] + zsem + zsem
        + [D((blocks, NM - 1))] * 2 + [D((blocks, NY - 1))] * 2,
        compiler_params=pltpu.CompilerParams(collective_id=0, has_side_effects=True),
        name="attention_backward",
    )(queries.reshape(nat), keys.reshape(nat), values.reshape(nat),
      norm_gain.reshape(1, HEAD_DIM), out_grad.reshape(nat))
    return tuple(o.reshape(tokens, HEAD_DIM) for o in out)


def solution(mesh):
    return jax.shard_map(
        per_device,
        mesh=mesh,
        in_specs=(
            P("ctx", "head"),
            P("ctx", "head"),
            P("ctx", "head"),
            P("head"),
            P("ctx", "head"),
        ),
        out_specs=(P("ctx", "head"), P("ctx", "head"), P("ctx", "head")),
        check_vma=False,
    )
```

time: 335 us -> 60.4 us (0.18)
  the two profiles are of different devices: /device:TPU:64 before, /device:TPU:8 now
where the time goes in v1:
time: 60.4 us; the launch traced here: 60.1 us
  Pallas kernels  55.5 us (92%)
  local copies, waits for them, and re-layouts  3.95 us (7%)
  between operations  0.65 us (1%)
    pallas_call x1, Pallas kernels, per_device(): pl.pallas_call(lambda *refs: kernel(blocks, width, *refs), out_shape=[jax...  55.5 us
    unnamed x7, local copies, waits for them, and re-layouts  3.95 us

profile of v1, /device:TPU:8, one launch (start us, length us, event | category | flops | bytes accessed | tf_op | source)
XLA Modules:
  0.0 60.1 jit_solution(2497300136540895398)
XLA Ops:
  0.6 55.5 %attention_backward.1 = (bf16[4,512,128]{2,1,0:T(8,128)(2,1)}, bf16[4,512,128]{2,1,0:T(8,128)(2,1)}, bf16[4,512,128]{2,1,0:T(8,128)(2,1)}) custom-call(bf16[4,512,128]{2,1,0:T(8,128)(2,1)} %bitcast.8, bf16[4,512,128]{2,1,0:T(8,128)(2,1)} %bitcast.9, bf16[4,512,128]{2,1,0:T(8,128)(2,1)} %bitcast.10, f32[1,128]{1,0:T(1,128)} %bitcast.15, ...), custom_call_target="tpu_custom_call" | custom-call | tf_op jit(solution)/shard_map/attention_backward/pallas_call | solution.py:259
  56.2 0.0 copy-start.1
  56.2 1.9 %copy.11 = bf16[2048,128]{1,0:T(8,128)(2,1)} copy(bf16[2048,128]{1,0:T(8,128)(2,1)} %bitcast.14) | data formatting | bytes 1048576
  58.1 0.0 copy-done.1
  58.1 0.0 copy-start
  58.1 0.8 %copy.12 = bf16[2048,128]{1,0:T(8,128)(2,1)} copy(bf16[2048,128]{1,0:T(8,128)(2,1)S(1)} %bitcast.13) | data formatting | bytes 1048576
  58.9 0.4 copy-done
  59.3 0.8 %copy.13 = bf16[2048,128]{1,0:T(8,128)(2,1)} copy(bf16[2048,128]{1,0:T(8,128)(2,1)S(1)} %bitcast.12) | data formatting | bytes 1048576
Async XLA Ops:
  56.2 1.9 %copy-start.1 = (bf16[4,512,128]{2,1,0:T(8,128)(2,1)S(1)}, bf16[4,512,128]{2,1,0:T(8,128)(2,1)}, u32[]{:S(2)}) copy-start(bf16[4,512,128]{2,1,0:T(8,128)(2,1)} %get-tuple-element.7) | copy-start | bytes 1572868
  58.1 1.2 %copy-start = (bf16[4,512,128]{2,1,0:T(8,128)(2,1)S(1)}, bf16[4,512,128]{2,1,0:T(8,128)(2,1)}, u32[]{:S(2)}) copy-start(bf16[4,512,128]{2,1,0:T(8,128)(2,1)} %get-tuple-element.8) | copy-start | bytes 1572868

commit v2 on v1

--- a/solution.py
+++ b/solution.py
@@ -13,6 +13,8 @@
 ARC = 4
 ROWS = HEAD_DIM // ARC
 MESH = pl.DeviceIdType.MESH
+KEPT = pltpu.VMEM
+VMEM_LIMIT = 40 * 1024 * 1024
 F32 = jnp.float32
 BF16 = jnp.bfloat16
 FAR_FIRST = (6, 5, 7, 4, 8, 3, 9, 2, 10, 1, 11)
@@ -39,6 +41,15 @@
 
     def before(self, i, j):
         return i < j if self.earlier else i > j
+
+    def needed(self, owner, to):
+        found = self.before(owner, to)
+        for off in NEAR:
+            found = jnp.logical_or(found, self.before((owner - off + NZ) % NZ, to))
+        return found
+
+    def from_(self, t):
+        return self.needed((self.z - t + NZ) % NZ, self.z)
 
     def first(self):
         copies = []
@@ -79,22 +90,25 @@
                 total = total + jnp.where(self.before(i, to), piece, 0.0)
             self.out[t] = total
             if t:
-                self.c2[n].start()
+                pl.when(self.needed(self.z, to))(self.c2[n].start)
 
     def finish(self, result):
-        for copy in self.c2:
-            copy.wait()
+        for t, copy in zip(FAR_FIRST, self.c2):
+            pl.when(self.needed(self.z, (self.z + t) % NZ))(copy.wait_send)
+            pl.when(self.from_(t))(copy.wait_recv)
         for r in range(ARC):
-            first = self.out[0] if r == 0 else self.inb[r]
-            result[(self.z - r + NZ) % ARC] = first + self.inb[r + 4] + (self.inb[r + 8])
-
-
-def kernel(blocks, width, q_hbm, k_hbm, v_hbm, gain_ref, og_hbm, qg_hbm, kg_hbm, vg_hbm,
-           q, k, v, og, qg, kg, vg, vt, kt, ut, at, sct, agt, ag, kgf, vgf,
-           kvt, sth, stl, st, stdh, stdl, adj, ext,
+            total = jnp.zeros((ROWS, HEAD_DIM), F32)
+            for t in range(r, NZ, ARC):
+                total = total + (jnp.where(self.from_(t), self.inb[t], 0.0) if t else self.out[0])
+            result[(self.z - r + NZ) % ARC] = total
+
+
+def kernel(blocks, width, q_hbm, k_hbm, v_hbm, gain_hbm, og_hbm,
+           qg, kgf, vgf, k, v, adjh, adjl,
+           q, og, gain_ref, vt, kt, ut, at, sct, agt, ag, kvt, st, stdh, stdl, adj, ext,
            src1, near1, out1, in1, src2, near2, out2, in2,
            stat, mstat, xin, yin,
-           lsem, osem, s11, r11, s12, r12, s21, r21, s22, r22, sx, rx, sy, ry):
+           lsem, greet, s11, r11, s12, r12, s21, r21, s22, r22, sx, rx, sy, ry):
     z = lax.axis_index("ctx")
     head = lax.axis_index("head")
     core = head % NC
@@ -103,7 +117,7 @@
     m = x * NC + core
 
     loads = [pltpu.make_async_copy(a, b, lsem.at[n])
-             for n, (a, b) in enumerate(((k_hbm, k), (v_hbm, v), (q_hbm, q), (og_hbm, og)))]
+             for n, (a, b) in enumerate(((k_hbm, k), (v_hbm, v), (q_hbm, q), (og_hbm, og), (gain_hbm, gain_ref)))]
     for copy in loads:
         copy.start()
 
@@ -114,10 +128,16 @@
         xpeers.append(((to // NC) * NY + y) * NC + to % NC)
     for d in range(1, NY):
         ypeers.append((x * NY + (y + d) % NY) * NC + core)
-    for t in FAR_FIRST:
-        pl.semaphore_signal(barrier, inc=1, device_id=((z + t) % NZ, head), device_id_type=MESH)
-    for to in ypeers + xpeers:
+    znear = [(z + d + NZ) % NZ for d in (1, -1, 2, -2)]
+    ynear = [ypeers[d - 1] for d in sorted({d % NY for d in (1, -1, 2, -2)} - {0})]
+    for to in znear:
+        pl.semaphore_signal(barrier, inc=1, device_id=(to, head), device_id_type=MESH)
+    for to in xpeers + ynear:
         pl.semaphore_signal(barrier, inc=1, device_id=(z, to), device_id_type=MESH)
+
+    def pass_on_z(n):
+        for to in znear[2:]:
+            pl.semaphore_signal(greet.at[n], inc=1, device_id=(to, head), device_id_type=MESH)
 
     loads[0].wait()
     loads[1].wait()
@@ -128,13 +148,18 @@
         total = total + dot(vt[n], k[n])
     src1[...] = total.reshape(ARC, ROWS, HEAD_DIM)
 
-    pl.semaphore_wait(barrier, NZ - 1 + NM - 1 + NY - 1)
+    pl.semaphore_wait(barrier, len(znear) + len(xpeers) + len(ynear))
     scan1 = Scan(z, head, True, (src1, near1, out1, in1, s11, r11, s12, r12))
     scan1.start()
+    pass_on_z(0)
+    if NY > 5:
+        for d in (2, NY - 2):
+            pl.semaphore_signal(greet.at[2], inc=1, device_id=(z, ypeers[d - 1]), device_id_type=MESH)
 
     row = lax.broadcasted_iota(jnp.int32, (GROUP, GROUP), 0)
     col = lax.broadcasted_iota(jnp.int32, (GROUP, GROUP), 1)
     keep = row <= col
+    loads[4].wait()
     gain = gain_ref[...]
 
     def local_scores(n):
@@ -149,9 +174,13 @@
     loads[3].wait()
     for n in range(blocks // 2):
         local_scores(n)
+    pl.semaphore_wait(greet.at[0], 2)
+    pass_on_z(1)
+    for n in range(blocks // 2, blocks - 1):
+        local_scores(n)
+    pl.semaphore_wait(greet.at[1], 2)
     scan1.forward()
-    for n in range(blocks // 2, blocks):
-        local_scores(n)
+    local_scores(blocks - 1)
     for n in range(blocks):
         local_rest(n)
     scan1.finish(ext)
@@ -177,6 +206,8 @@
                 device_id=(z, xpeers[d - 1]), device_id_type=MESH)
             copy.start()
             xcopies.append(copy)
+    if NY > 5:
+        pl.semaphore_wait(greet.at[2], 2)
     for n in range(blocks):
         total = stat[n]
         for d in range(1, NM):
@@ -225,21 +256,25 @@
     scan2.forward()
     for n in range(blocks // 2, blocks):
         local_grads(n)
-    out_q = pltpu.make_async_copy(qg, qg_hbm, osem.at[0])
-    out_q.start()
     scan2.finish(ext)
     later = ext[...].reshape(HEAD_DIM, HEAD_DIM)
     for n in range(blocks):
-        hi, lo = split(later + adj[n])
+        adjh[n], adjl[n] = split(later + adj[n])
+
+
+def finish(blocks, qg, kgf, vgf, k, v, adjh, adjl, qg_hbm, kg_hbm, vg_hbm, kg, vg, sem):
+    copies = [pltpu.make_async_copy(qg, qg_hbm, sem.at[0, blocks])]
+    copies[0].start()
+    for n in range(blocks):
+        hi, lo = adjh[n], adjl[n]
         kg[n] = (kgf[n] + dot(v[n], hi) + dot(v[n], lo)).astype(BF16)
+        copies.append(pltpu.make_async_copy(kg.at[n], kg_hbm.at[n], sem.at[0, n]))
+        copies[-1].start()
         vg[n] = (vgf[n] + dot_nt(k[n], hi) + dot_nt(k[n], lo)).astype(BF16)
-    out_k = pltpu.make_async_copy(kg, kg_hbm, osem.at[1])
-    out_v = pltpu.make_async_copy(vg, vg_hbm, osem.at[2])
-    out_k.start()
-    out_v.start()
-    out_q.wait()
-    out_k.wait()
-    out_v.wait()
+        copies.append(pltpu.make_async_copy(vg.at[n], vg_hbm.at[n], sem.at[1, n]))
+        copies[-1].start()
+    for copy in copies:
+        copy.wait()
 
 
 def per_device(queries, keys, values, norm_gain, out_grad):
@@ -256,25 +291,38 @@
     zbuf = [V((ARC, *piece), F32), V((len(NEAR), *piece), F32), V((NZ, *piece), F32), V((NZ, *piece), F32)]
     zsem = [D((len(NEAR),)), D((len(NEAR),)), D((NZ,)), D((NZ,))]
     anyspec = pl.BlockSpec(memory_space=pl.ANY)
+    hbmspec = pl.BlockSpec(memory_space=pltpu.HBM)
+    vspec = pl.BlockSpec(memory_space=pltpu.VMEM)
     out = pl.pallas_call(
         lambda *refs: kernel(blocks, width, *refs),
-        out_shape=[jax.ShapeDtypeStruct(nat, BF16)] * 3,
-        in_specs=[anyspec] * 3 + [pl.BlockSpec(memory_space=pltpu.VMEM)] + [anyspec],
-        out_specs=[anyspec] * 3,
-        scratch_shapes=[V(nat, BF16)] * 7
-        + [V(tra, BF16), V(tra, BF16), V(tra, F32), V(tra, F32), V((blocks, GROUP, GROUP), BF16),
-           V(tra, BF16), V(nat, BF16), V(nat, F32), V(nat, F32),
-           V(sq, F32), V(sq, BF16), V(sq, BF16), V(sq, F32), V(sq, BF16), V(sq, BF16), V(sq, F32),
+        out_shape=[KEPT(nat, BF16), KEPT(nat, F32), KEPT(nat, F32), KEPT(nat, BF16), KEPT(nat, BF16),
+                   KEPT(sq, BF16), KEPT(sq, BF16)],
+        in_specs=[hbmspec] * 5,
+        out_specs=[vspec] * 7,
+        scratch_shapes=[V(nat, BF16)] * 2
+        + [V((1, HEAD_DIM), F32), V(tra, BF16), V(tra, BF16), V(tra, F32), V(tra, F32), V((blocks, GROUP, GROUP), BF16),
+           V(tra, BF16), V(nat, BF16),
+           V(sq, F32), V(sq, F32), V(sq, BF16), V(sq, BF16), V(sq, F32),
            V((ARC, *piece), F32)]
         + zbuf + zbuf
         + [V((blocks, srows, HEAD_DIM), F32), V((blocks, srows, HEAD_DIM), F32),
            V((blocks, NM - 1, srows, HEAD_DIM), F32), V((blocks, NY - 1, srows, HEAD_DIM), F32)]
-        + [D((4,)), D((3,))] + zsem + zsem
+        + [D((5,)), pltpu.SemaphoreType.REGULAR((3,))] + zsem + zsem
         + [D((blocks, NM - 1))] * 2 + [D((blocks, NY - 1))] * 2,
-        compiler_params=pltpu.CompilerParams(collective_id=0, has_side_effects=True),
+        compiler_params=pltpu.CompilerParams(collective_id=0, has_side_effects=True, vmem_limit_bytes=VMEM_LIMIT),
         name="attention_backward",
-    )(queries.reshape(nat), keys.reshape(nat), values.reshape(nat),
-      norm_gain.reshape(1, HEAD_DIM), out_grad.reshape(nat))
+    )(*(pltpu.with_memory_space_constraint(a.reshape(nat), pltpu.HBM) for a in (queries, keys, values)),
+      pltpu.with_memory_space_constraint(norm_gain.reshape(1, HEAD_DIM), pltpu.HBM),
+      pltpu.with_memory_space_constraint(out_grad.reshape(nat), pltpu.HBM))
+    out = pl.pallas_call(
+        lambda *refs: finish(blocks, *refs),
+        out_shape=[jax.ShapeDtypeStruct(nat, BF16)] * 3,
+        in_specs=[vspec] * 7,
+        out_specs=[anyspec] * 3,
+        scratch_shapes=[V(nat, BF16)] * 2 + [D((2, blocks + 1))],
+        compiler_params=pltpu.CompilerParams(vmem_limit_bytes=VMEM_LIMIT // 4),
+        name="finish",
+    )(*(pltpu.with_memory_space_constraint(o, pltpu.VMEM) for o in out))
     return tuple(o.reshape(tokens, HEAD_DIM) for o in out)
 
 

time: 60.4 us -> 54.6 us (0.904)
  local copies, waits for them, and re-layouts: 3.95 us -> 0 us
  Pallas kernels: 55.5 us -> 53.8 us
    unnamed x7 -> x0, local copies, waits for them, and re-layouts: 3.95 us -> none
    pallas_call x1 -> x2, Pallas kernels: 55.5 us -> 53.8 us  [the longest x1 52.4 us: per_device(): pl.pallas_call(lambda *refs: kernel(blocks, width, *refs), out_shape=[KEP...]
where the time goes in v2:
time: 54.6 us; the launch traced here: 54.5 us
  Pallas kernels  53.8 us (99%)
  between operations  0.64 us (1%)
    pallas_call x1, Pallas kernels, per_device(): pl.pallas_call(lambda *refs: kernel(blocks, width, *refs), out_shape=[KEP...  52.4 us
    pallas_call x1, Pallas kernels, per_device(): pl.pallas_call(lambda *refs: finish(blocks, *refs), out_shape=[jax.ShapeD...  1.48 us

profile of v2, /device:TPU:8, one launch (start us, length us, event | category | flops | bytes accessed | tf_op | source)
XLA Modules:
  0.0 54.5 jit_solution(15746381018008332142)
XLA Ops:
  0.6 52.4 %attention_backward.1 = (bf16[4,512,128]{2,1,0:T(8,128)(2,1)S(1)}, f32[4,512,128]{2,1,0:T(8,128)S(1)}, f32[4,512,128]{2,1,0:T(8,128)S(1)}, bf16[4,512,128]{2,1,0...) custom-call(bf16[4,512,128]{2,1,0:T(8,128)(2,1)} %bitcast.8, ...), custom_call_target="tpu_custom_call" | custom-call | tf_op jit(solution)/shard_map/attention_backward/pallas_call | solution.py:296
  53.0 1.5 %finish.1 = (bf16[4,512,128]{2,1,0:T(8,128)(2,1)}, bf16[4,512,128]{2,1,0:T(8,128)(2,1)}, bf16[4,512,128]{2,1,0:T(8,128)(2,1)}) custom-call(bf16[4,512,128]{2,1,0:T(8,128)(2,1)S(1)} %get-tuple-element.13.refs_0_, f32[4,512,128]{2,1,0:T(8,128)S(1)} %get-tuple-element.14.refs_1_, f32[4,512,128]{2,1,0:T(8,128)S(1)} %get-tuple-element.15.refs_2_, ...), custom_call_target="tpu_custom_call" | custom-call | tf_op jit(solution)/shard_map/finish/pallas_call | solution.py:317

commit v3 on v2

--- a/solution.py
+++ b/solution.py
@@ -17,8 +17,6 @@
 VMEM_LIMIT = 40 * 1024 * 1024
 F32 = jnp.float32
 BF16 = jnp.bfloat16
-FAR_FIRST = (6, 5, 7, 4, 8, 3, 9, 2, 10, 1, 11)
-NEAR = (2, 1, -1)
 
 
 def dot(a, b):
@@ -35,72 +33,115 @@
 
 
 class Scan:
-    def __init__(self, z, head, earlier, refs):
-        self.z, self.head, self.earlier = z, head, earlier
+    def __init__(self, z, head, step, refs):
+        self.z, self.head, self.step, self.c2 = z, head, step, {}
+        self.group, self.place = z // ARC, z % ARC
+        self.end = NZ - 1 if step > 0 else 0
         self.src, self.near, self.out, self.inb, self.s1, self.r1, self.s2, self.r2 = refs
 
-    def before(self, i, j):
-        return i < j if self.earlier else i > j
-
-    def needed(self, owner, to):
-        found = self.before(owner, to)
-        for off in NEAR:
-            found = jnp.logical_or(found, self.before((owner - off + NZ) % NZ, to))
-        return found
-
-    def from_(self, t):
-        return self.needed((self.z - t + NZ) % NZ, self.z)
-
-    def first(self):
-        copies = []
-        for n, off in enumerate(NEAR):
-            to = (self.z + off + NZ) % NZ
-            copies.append(pltpu.make_async_remote_copy(
-                src_ref=self.src.at[to % ARC], dst_ref=self.near.at[n],
-                send_sem=self.s1.at[n], recv_sem=self.r1.at[n],
-                device_id=(to, self.head), device_id_type=MESH))
-        return copies
-
-    def second(self):
-        copies = []
-        for t in FAR_FIRST:
-            to = (self.z + t) % NZ
-            copies.append(pltpu.make_async_remote_copy(
-                src_ref=self.out.at[t], dst_ref=self.inb.at[t],
-                send_sem=self.s2.at[t], recv_sem=self.r2.at[t],
-                device_id=(to, self.head), device_id_type=MESH))
-        return copies
+    def mate(self, off):
+        return self.group * ARC + (self.place + off + ARC) % ARC
+
+    def copy(self, src, dst, send, recv, to):
+        return pltpu.make_async_remote_copy(
+            src_ref=src, dst_ref=dst, send_sem=send, recv_sem=recv, device_id=(to, self.head), device_id_type=MESH)
 
     def start(self):
-        self.c1 = self.first()
+        self.c1 = [self.copy(self.src.at[(self.place + off) % ARC], self.near.at[off - 1],
+                             self.s1.at[off - 1], self.r1.at[off - 1], self.mate(off)) for off in range(1, ARC)]
         for copy in self.c1:
-            copy.start()
-
-    def forward(self):
-        for copy in self.c1:
+            pl.when(self.z != self.end)(copy.start)
+
+    def gather(self):
+        for off, copy in enumerate(self.c1, 1):
+            pl.when(self.z != self.end)(copy.wait_send)
+            pl.when(self.mate(-off) != self.end)(copy.wait_recv)
+        return [(self.z, self.src[self.place])] + [(self.mate(-off), self.near[off - 1]) for off in range(1, ARC)]
+
+    def before(self, i, to):
+        return i < to if self.step > 0 else i > to
+
+    def there(self, k):
+        to = self.group + self.step * k
+        return jnp.logical_and(to >= 0, to < NZ // ARC)
+
+    def pass_on(self, greet):
+        self.mine = self.gather()
+        total = jnp.zeros((ROWS, HEAD_DIM), F32)
+        for _, piece in self.mine:
+            total = total + piece
+        self.out[ARC] = total
+        self.on = {}
+        for k in range(1, NZ // ARC):
+            to = (self.z + self.step * ARC * k + NZ) % NZ
+            self.on[k] = self.copy(self.out.at[ARC], self.inb.at[ARC + k], self.s2.at[ARC + k], self.r2.at[ARC + k], to)
+
+            @pl.when(self.there(k))
+            def _():
+                pl.semaphore_wait(greet.at[k], 1)
+                self.on[k].start()
+
+    def share(self):
+        before = jnp.zeros((ROWS, HEAD_DIM), F32)
+        for k in range(1, NZ // ARC):
+            pl.when(self.there(-k))(self.on[k].wait_recv)
+            before = before + jnp.where(self.there(-k), self.inb[ARC + k], 0.0)
+        self.c2 = []
+        for off in range(ARC):
+            total = before
+            for i, piece in self.mine:
+                total = total + jnp.where(self.before(i, self.mate(off)), piece, 0.0)
+            self.out[off] = total
+            if off:
+                self.c2.append(self.copy(self.out.at[off], self.inb.at[off],
+                                         self.s2.at[off], self.r2.at[off], self.mate(off)))
+                self.c2[-1].start()
+
+    def finish(self, result):
+        result[self.place] = self.out[0]
+        for off, copy in enumerate(self.c2, 1):
             copy.wait()
-        mine = [(self.z, self.src[self.z % ARC])]
-        for n, off in enumerate(NEAR):
-            mine.append(((self.z - off + NZ) % NZ, self.near[n]))
-        self.c2 = self.second()
-        for n, t in enumerate((*FAR_FIRST, 0)):
-            to = (self.z + t) % NZ
+            result[(self.place - off + ARC) % ARC] = self.inb[off]
+
+    def close(self):
+        for k, copy in self.on.items():
+            pl.when(self.there(k))(copy.wait_send)
+
+
+class AdjointScan(Scan):
+    def targets(self, k):
+        for place in range(ARC):
+            to = ((self.group + self.step * k + NZ) % (NZ // ARC)) * ARC + place
+            sends = self.place != place if k == 0 else self.there(k)
+            yield k * ARC + place, to, sends
+
+    def spread(self, k, mine):
+        for n, to, sends in self.targets(k):
             total = jnp.zeros((ROWS, HEAD_DIM), F32)
             for i, piece in mine:
-                total = total + jnp.where(self.before(i, to), piece, 0.0)
-            self.out[t] = total
-            if t:
-                pl.when(self.needed(self.z, to))(self.c2[n].start)
+                total = total + (jnp.where(self.before(i, to), piece, 0.0) if k == 0 else piece)
+            self.out[n] = total
+            self.c2[n] = self.copy(self.out.at[n], self.inb.at[self.z], self.s2.at[n], self.r2.at[self.z], to)
+            pl.when(sends)(self.c2[n].start)
+
+    def crosses(self, owner, to):
+        between = to // ARC - owner // ARC
+        return jnp.logical_and(owner != to, (between if self.step > 0 else -between) >= 0)
 
     def finish(self, result):
-        for t, copy in zip(FAR_FIRST, self.c2):
-            pl.when(self.needed(self.z, (self.z + t) % NZ))(copy.wait_send)
-            pl.when(self.from_(t))(copy.wait_recv)
+        for o in range(NZ):
+            arrival = self.copy(self.out.at[0], self.inb.at[o], self.s2.at[0], self.r2.at[o], jnp.int32(o))
+            pl.when(self.crosses(o, self.z))(arrival.wait_recv)
         for r in range(ARC):
-            total = jnp.zeros((ROWS, HEAD_DIM), F32)
-            for t in range(r, NZ, ARC):
-                total = total + (jnp.where(self.from_(t), self.inb[t], 0.0) if t else self.out[0])
-            result[(self.z - r + NZ) % ARC] = total
+            total = jnp.where(self.place == r, self.out[self.place], 0.0)
+            for o in range(r, NZ, ARC):
+                total = total + jnp.where(self.crosses(o, self.z), self.inb[o], 0.0)
+            result[r] = total
+
+    def close(self):
+        for k in range(NZ // ARC):
+            for n, _, sends in self.targets(k):
+                pl.when(sends)(self.c2[n].wait_send)
 
 
 def kernel(blocks, width, q_hbm, k_hbm, v_hbm, gain_hbm, og_hbm,
@@ -128,33 +169,42 @@
         xpeers.append(((to // NC) * NY + y) * NC + to % NC)
     for d in range(1, NY):
         ypeers.append((x * NY + (y + d) % NY) * NC + core)
-    znear = [(z + d + NZ) % NZ for d in (1, -1, 2, -2)]
+    scan1 = Scan(z, head, 1, (src1, near1, out1, in1, s11, r11, s12, r12))
+    scan2 = AdjointScan(z, head, -1, (src2, near2, out2, in2, s21, r21, s22, r22))
     ynear = [ypeers[d - 1] for d in sorted({d % NY for d in (1, -1, 2, -2)} - {0})]
-    for to in znear:
-        pl.semaphore_signal(barrier, inc=1, device_id=(to, head), device_id_type=MESH)
+    for off in range(1, ARC):
+        pl.semaphore_signal(barrier, inc=1, device_id=(scan1.mate(off), head), device_id_type=MESH)
+
+    for g in range(1, NZ // ARC):
+        @pl.when(scan1.there(g))
+        def _():
+            pl.semaphore_signal(barrier, inc=1, device_id=((z + ARC * g) % NZ, head), device_id_type=MESH)
+
     for to in xpeers + ynear:
         pl.semaphore_signal(barrier, inc=1, device_id=(z, to), device_id_type=MESH)
 
-    def pass_on_z(n):
-        for to in znear[2:]:
-            pl.semaphore_signal(greet.at[n], inc=1, device_id=(to, head), device_id_type=MESH)
-
-    loads[0].wait()
-    loads[1].wait()
-    total = jnp.zeros((HEAD_DIM, HEAD_DIM), F32)
-    for n in range(blocks):
-        vt[n] = v[n].T
-        kvt[n] = total
-        total = total + dot(vt[n], k[n])
-    src1[...] = total.reshape(ARC, ROWS, HEAD_DIM)
-
-    pl.semaphore_wait(barrier, len(znear) + len(xpeers) + len(ynear))
-    scan1 = Scan(z, head, True, (src1, near1, out1, in1, s11, r11, s12, r12))
+    def products():
+        loads[0].wait()
+        loads[1].wait()
+        total = jnp.zeros((HEAD_DIM, HEAD_DIM), F32)
+        for n in range(blocks):
+            vt[n] = v[n].T
+            kvt[n] = total
+            total = total + dot(vt[n], k[n])
+        src1[...] = total.reshape(ARC, ROWS, HEAD_DIM)
+
+    pl.when(z < NZ - 1)(products)
+    pl.semaphore_wait(barrier, z // ARC + (ARC - 1 + len(xpeers) + len(ynear)))
+    for g in range(1, NZ // ARC):
+        @pl.when(scan2.there(g))
+        def _():
+            pl.semaphore_signal(greet.at[g], inc=1, device_id=((z + NZ - ARC * g) % NZ, head), device_id_type=MESH)
+
+    pl.when(z == NZ - 1)(products)
     scan1.start()
-    pass_on_z(0)
     if NY > 5:
         for d in (2, NY - 2):
-            pl.semaphore_signal(greet.at[2], inc=1, device_id=(z, ypeers[d - 1]), device_id_type=MESH)
+            pl.semaphore_signal(greet.at[0], inc=1, device_id=(z, ypeers[d - 1]), device_id_type=MESH)
 
     row = lax.broadcasted_iota(jnp.int32, (GROUP, GROUP), 0)
     col = lax.broadcasted_iota(jnp.int32, (GROUP, GROUP), 1)
@@ -172,17 +222,12 @@
 
     loads[2].wait()
     loads[3].wait()
-    for n in range(blocks // 2):
+    for n in range(blocks):
         local_scores(n)
-    pl.semaphore_wait(greet.at[0], 2)
-    pass_on_z(1)
-    for n in range(blocks // 2, blocks - 1):
-        local_scores(n)
-    pl.semaphore_wait(greet.at[1], 2)
-    scan1.forward()
-    local_scores(blocks - 1)
     for n in range(blocks):
         local_rest(n)
+    scan1.pass_on(greet)
+    scan1.share()
     scan1.finish(ext)
 
     tiles = GROUP // HEAD_DIM
@@ -207,7 +252,7 @@
             copy.start()
             xcopies.append(copy)
     if NY > 5:
-        pl.semaphore_wait(greet.at[2], 2)
+        pl.semaphore_wait(greet.at[0], 2)
     for n in range(blocks):
         total = stat[n]
         for d in range(1, NM):
@@ -240,7 +285,6 @@
         adj[n] = suffix
         suffix = suffix + own
     src2[...] = suffix.reshape(ARC, ROWS, HEAD_DIM)
-    scan2 = Scan(z, head, False, (src2, near2, out2, in2, s21, r21, s22, r22))
     scan2.start()
 
     def local_grads(n):
@@ -253,13 +297,17 @@
 
     for n in range(blocks // 2):
         local_grads(n)
-    scan2.forward()
+    mine = scan2.gather()
+    for g in reversed(range(NZ // ARC)):
+        scan2.spread(g, mine)
     for n in range(blocks // 2, blocks):
         local_grads(n)
     scan2.finish(ext)
     later = ext[...].reshape(HEAD_DIM, HEAD_DIM)
     for n in range(blocks):
         adjh[n], adjl[n] = split(later + adj[n])
+    scan1.close()
+    scan2.close()
 
 
 def finish(blocks, qg, kgf, vgf, k, v, adjh, adjl, qg_hbm, kg_hbm, vg_hbm, kg, vg, sem):
@@ -288,8 +336,8 @@
     D = pltpu.SemaphoreType.DMA
     piece = (ROWS, HEAD_DIM)
     srows = 2 * GROUP // HEAD_DIM
-    zbuf = [V((ARC, *piece), F32), V((len(NEAR), *piece), F32), V((NZ, *piece), F32), V((NZ, *piece), F32)]
-    zsem = [D((len(NEAR),)), D((len(NEAR),)), D((NZ,)), D((NZ,))]
+    zbuf = [V((ARC, *piece), F32), V((ARC - 1, *piece), F32), V((NZ, *piece), F32), V((NZ, *piece), F32)]
+    zsem = [D((ARC - 1,)), D((ARC - 1,)), D((NZ,)), D((NZ,))]
     anyspec = pl.BlockSpec(memory_space=pl.ANY)
     hbmspec = pl.BlockSpec(memory_space=pltpu.HBM)
     vspec = pl.BlockSpec(memory_space=pltpu.VMEM)
@@ -307,7 +355,7 @@
         + zbuf + zbuf
         + [V((blocks, srows, HEAD_DIM), F32), V((blocks, srows, HEAD_DIM), F32),
            V((blocks, NM - 1, srows, HEAD_DIM), F32), V((blocks, NY - 1, srows, HEAD_DIM), F32)]
-        + [D((5,)), pltpu.SemaphoreType.REGULAR((3,))] + zsem + zsem
+        + [D((5,)), pltpu.SemaphoreType.REGULAR((NZ // ARC,))] + zsem + zsem
         + [D((blocks, NM - 1))] * 2 + [D((blocks, NY - 1))] * 2,
         compiler_params=pltpu.CompilerParams(collective_id=0, has_side_effects=True, vmem_limit_bytes=VMEM_LIMIT),
         name="attention_backward",

time: 54.6 us -> 52.3 us (0.958)
  Pallas kernels: 53.8 us -> 51.5 us
    pallas_call x1, Pallas kernels: 52.4 us -> 50 us  [per_device(): pl.pallas_call(lambda *refs: kernel(blocks, width, *refs), out_shape=[KEP...]
where the time goes in v3:
time: 52.3 us; the launch traced here: 52.1 us
  Pallas kernels  51.5 us (98%)
  between operations  0.64 us (1%)
    pallas_call x1, Pallas kernels, per_device(): pl.pallas_call(lambda *refs: kernel(blocks, width, *refs), out_shape=[KEP...  50 us
    pallas_call x1, Pallas kernels, per_device(): pl.pallas_call(lambda *refs: finish(blocks, *refs), out_shape=[jax.ShapeD...  1.47 us

profile of v3, /device:TPU:8, one launch (start us, length us, event | category | flops | bytes accessed | tf_op | source)
XLA Modules:
  0.0 52.1 jit_solution(3427256898805140087)
XLA Ops:
  0.6 50.0 %attention_backward.1 = (bf16[4,512,128]{2,1,0:T(8,128)(2,1)S(1)}, f32[4,512,128]{2,1,0:T(8,128)S(1)}, f32[4,512,128]{2,1,0:T(8,128)S(1)}, bf16[4,512,128]{2,1,0...) custom-call(bf16[4,512,128]{2,1,0:T(8,128)(2,1)} %bitcast.8, ...), custom_call_target="tpu_custom_call" | custom-call | tf_op jit(solution)/shard_map/attention_backward/pallas_call | solution.py:344
  50.7 1.5 %finish.1 = (bf16[4,512,128]{2,1,0:T(8,128)(2,1)}, bf16[4,512,128]{2,1,0:T(8,128)(2,1)}, bf16[4,512,128]{2,1,0:T(8,128)(2,1)}) custom-call(bf16[4,512,128]{2,1,0:T(8,128)(2,1)S(1)} %get-tuple-element.13.refs_0_, f32[4,512,128]{2,1,0:T(8,128)S(1)} %get-tuple-element.14.refs_1_, f32[4,512,128]{2,1,0:T(8,128)S(1)} %get-tuple-element.15.refs_2_, ...), custom_call_target="tpu_custom_call" | custom-call | tf_op jit(solution)/shard_map/finish/pallas_call | solution.py:365

commit v4 on v3

--- a/solution.py
+++ b/solution.py
@@ -232,7 +232,7 @@
 
     tiles = GROUP // HEAD_DIM
     earlier = ext[...].reshape(HEAD_DIM, HEAD_DIM)
-    xcopies, ycopies = [], {}
+    xcopies, ycopies = {}, {}
     for n in range(blocks):
         state = earlier + kvt[n]
         st[n] = state
@@ -244,19 +244,19 @@
         for c in range(tiles):
             stat[n, c : c + 1, :] = power[:, c * HEAD_DIM : (c + 1) * HEAD_DIM]
             stat[n, tiles + c : tiles + c + 1, :] = cross[:, c * HEAD_DIM : (c + 1) * HEAD_DIM]
-        for d in range(1, NM):
+        for d in sorted(range(1, NM), key=lambda d: -min(d, NM - d)):
             copy = pltpu.make_async_remote_copy(
                 src_ref=stat.at[n], dst_ref=xin.at[n, d - 1],
                 send_sem=sx.at[n, d - 1], recv_sem=rx.at[n, d - 1],
                 device_id=(z, xpeers[d - 1]), device_id_type=MESH)
             copy.start()
-            xcopies.append(copy)
+            xcopies[n, d] = copy
     if NY > 5:
         pl.semaphore_wait(greet.at[0], 2)
     for n in range(blocks):
         total = stat[n]
         for d in range(1, NM):
-            xcopies[n * (NM - 1) + d - 1].wait()
+            xcopies[n, d].wait()
             total = total + xin[n, d - 1]
         mstat[n] = total
         for d in sorted(range(1, NY), key=lambda d: -min(d, NY - d)):

time: 52.3 us -> 52.2 us (level)
  no operation moved by 1% of the time
where the time goes in v4:
time: 52.2 us; the launch traced here: 52 us
  Pallas kernels  51.4 us (98%)
  between operations  0.64 us (1%)
    pallas_call x1, Pallas kernels, per_device(): pl.pallas_call(lambda *refs: kernel(blocks, width, *refs), out_shape=[KEP...  49.9 us
    pallas_call x1, Pallas kernels, per_device(): pl.pallas_call(lambda *refs: finish(blocks, *refs), out_shape=[jax.ShapeD...  1.47 us

profile of v4, /device:TPU:8, one launch (start us, length us, event | category | flops | bytes accessed | tf_op | source)
XLA Modules:
  0.0 52.0 jit_solution(7440884581292086249)
XLA Ops:
  0.6 49.9 %attention_backward.1 = (bf16[4,512,128]{2,1,0:T(8,128)(2,1)S(1)}, f32[4,512,128]{2,1,0:T(8,128)S(1)}, f32[4,512,128]{2,1,0:T(8,128)S(1)}, bf16[4,512,128]{2,1,0...) custom-call(bf16[4,512,128]{2,1,0:T(8,128)(2,1)} %bitcast.8, ...), custom_call_target="tpu_custom_call" | custom-call | tf_op jit(solution)/shard_map/attention_backward/pallas_call | solution.py:344
  50.6 1.5 %finish.1 = (bf16[4,512,128]{2,1,0:T(8,128)(2,1)}, bf16[4,512,128]{2,1,0:T(8,128)(2,1)}, bf16[4,512,128]{2,1,0:T(8,128)(2,1)}) custom-call(bf16[4,512,128]{2,1,0:T(8,128)(2,1)S(1)} %get-tuple-element.13.refs_0_, f32[4,512,128]{2,1,0:T(8,128)S(1)} %get-tuple-element.14.refs_1_, f32[4,512,128]{2,1,0:T(8,128)S(1)} %get-tuple-element.15.refs_2_, ...), custom_call_target="tpu_custom_call" | custom-call | tf_op jit(solution)/shard_map/finish/pallas_call | solution.py:365
